TPU v7x, 128 devices: a whole 4x4x4 slice. The times are simulated.
128 devices in a mesh: mp: 4 (over z_lo, core), fsdp: 32 (over x, z_hi, y).
Axes of the slice: x: 4, y: 4, z: 4 (z_hi: 2, z_lo: 2; z = z_hi * 2 + z_lo), core: 2. Of those that a mesh axis runs over, the one named last changes fastest.
Arguments:
- activations: bfloat16 [4, 4096, 8192], P('mp', 'fsdp'), may hold values from -6 to 6
- out_grads: bfloat16 [4, 4096, 7168], P('mp', 'fsdp'), may hold values from -0.29882812 to 0.29882812
- seq_ids: int32 [4, 4096], P('mp', 'fsdp'), may hold values from 0 to 1, as said below
- weights: bfloat16 [4, 32768, 1792], P('mp', 'fsdp'), may hold values from -6 to 6
Outputs:
- merged: bfloat16 [32768, 1792], P('fsdp')
Inputs may be any that keep to these rules, and one draw needn't show every extreme that they name: `seq_ids`: sequence ids never fall along the tokens of a copy; in every copy one of the 2 sequences holds exactly 3072 neighbouring tokens and the other the remaining 4096 - 3072, in either order.
All inputs are finite; a program needn't handle non-finite values.
Results may differ from a plain program's by a relative error of at most 0.001.
Values may be sent and summed in bfloat16 or wider, within the bound.
A program may use at most 128 MiB of HBM per device.

v0:
```python
import jax
import jax.numpy as jnp
from jax import lax
from jax.sharding import PartitionSpec as P

F = 7168
SEQS = 2
smoothing = 0.05


def per_device(activations, out_grads, seq_ids, weights):
    devices = lax.axis_size("fsdp")
    col_width = weights.shape[2]
    row_width = weights.shape[1]
    blocks = F // col_width
    row_blocks = devices // blocks
    tok_local = activations.shape[1]
    act_blocks = activations[0].reshape(tok_local, row_blocks, row_width).transpose(1, 0, 2)
    act_send = jnp.tile(act_blocks, (blocks, 1, 1))
    grad_blocks = out_grads[0].reshape(tok_local, blocks, col_width).transpose(1, 0, 2)
    grad_send = jnp.repeat(grad_blocks, row_blocks, axis=0)
    act_all = lax.all_to_all(act_send, "fsdp", split_axis=0, concat_axis=1, tiled=True)[0]
    grad_all = lax.all_to_all(grad_send, "fsdp", split_axis=0, concat_axis=1, tiled=True)[0]
    owners = lax.all_gather(seq_ids[0], "fsdp", axis=0, tiled=True)
    total = owners.shape[0]
    longest = total // SEQS * 3 // 2

    def per_sequence(seq, fisher):
        first = jnp.sum((owners < seq).astype(jnp.int32))
        first = jnp.minimum(first, jnp.int32(total - longest))
        act_window = lax.dynamic_slice_in_dim(act_all, first, longest, 0)
        grad_window = lax.dynamic_slice_in_dim(grad_all, first, longest, 0)
        owner_window = lax.dynamic_slice_in_dim(owners, first, longest, 0)
        masked = jnp.where((owner_window == seq)[:, None], grad_window, jnp.zeros_like(grad_window))
        grad = lax.dot_general(
            act_window, masked, (((0,), (0,)), ((), ())), preferred_element_type=jnp.float32
        )
        return fisher + grad * grad

    fisher = lax.fori_loop(0, SEQS, per_sequence, jnp.zeros((row_width, col_width), jnp.float32))
    prior = fisher / SEQS + smoothing
    numer = prior * weights[0].astype(jnp.float32)
    numer_sum, denom_sum = lax.psum((numer, prior), "mp")
    merged = (numer_sum / denom_sum).astype(jnp.bfloat16)
    return merged


def solution(mesh):
    placed = (P("mp", "fsdp", None), P("mp", "fsdp", None), P("mp", "fsdp"), P("mp", "fsdp", None))
    return jax.shard_map(
        per_device, mesh=mesh, in_specs=placed, out_specs=P("fsdp", None), check_vma=False
    )
```

profile of v0, /device:TPU:1, one launch (start us, length us, event | category | flops | bytes accessed | tf_op | source)
XLA Modules:
  0.0 852.1 jit_solution(7776468837257482357)
XLA Ops:
  6.5 3.0 copy.7
  9.5 1.2 copy.5
  10.7 4.3 tile.4
  15.0 11.3 %all-to-all-start = ((bf16[32,128,1024]{2,1,0:T(8,128)(2,1)}), bf16[32,128,1024]{2,1,0:T(8,128)(2,1)}, u32[]{:S(2)}, u32[]{:S(2)}) async-start(bf16[32,128,1024]{2,1,0:T(8,128)(2,1)} %bitcast.15), calls=%async_computation | async-start | bytes 16777216 | tf_op jit(solution)/shard_map/all_to_all | solution.py:22
  26.4 3.6 reshape_squeeze.7
  30.0 1.4 copy.6
  31.4 148.4 %all-to-all-done = bf16[32,128,1024]{2,1,0:T(8,128)(2,1)} async-done(((bf16[32,128,1024]{2,1,0:T(8,128)(2,1)}), bf16[32,128,1024]{2,1,0:T(8,128)(2,1)}, u32[]{:S(2)}, u32[]{:S(2)}) %all-to-all-start) | async-done | bytes 8388640 | tf_op jit(solution)/shard_map/all_to_all | solution.py:22
  179.8 6.5 broadcast_in_dim.26
  186.3 0.0 copy-start
  186.3 13.4 %all-to-all-start.1 = ((bf16[32,128,1792]{2,1,0:T(8,128)(2,1)}), bf16[32,128,1792]{2,1,0:T(8,128)(2,1)}, u32[]{:S(2)}, u32[]{:S(2)}) async-start(bf16[32,128,1792]{2,1,0:T(8,128)(2,1)} %bitcast.14), calls=%async_computation.1 | async-start | bytes 29360128 | tf_op jit(solution)/shard_map/all_to_all | solution.py:23
  199.7 0.0 all-reduce.3.cloned.1.call-start
  199.8 0.0 copy-done
  199.8 301.8 %all-gather = s32[1,4096]{1,0:T(1,128)S(1)} all-gather(s32[1,128]{1,0:T(1,128)S(1)} %copy-done), channel_id=2, replica_groups=mesh['mp'=4,'fsdp'=32] {'fsdp'}, dimensions={1}, use_global_device_ids=true | all-gather | bytes 16896 | tf_op jit(solution)/shard_map/all_gather | solution.py:24
  501.6 0.0 all-to-all-done.1
  501.6 44.0 %while.14 = (s32[]{:T(128)}, f32[1024,1792]{1,0:T(8,128)}, s32[4096]{0:T(1024)S(1)}, bf16[4096,1024]{1,0:T(8,128)(2,1)}, bf16[4096,1792]{1,0:T(8,128)(2,1)}, /*index=5*/s32[]{:T(128)}, s32[]{:T(128)}, s32[]{:T(128)}, s32[]{:T(128)}) while((s32[]{:T(128)}, f32[1024,1792]{1,0:T(8,128)}, s32[4096]{0:T(1024)S(1)}, ...), condition=%wide.region_2.3_spmd.clone, body=%wide.region_0.2_spmd.clone.sunk | while | flops 11285314560 | bytes 32018084 | solution.py:40
  501.6 0.7 convert_reduce_fusion.2
  502.9 0.1 dynamic-slice_compare_fusion.2
  503.0 20.1 %select_add_fusion.2 = f32[1024,1792]{1,0:T(8,128)} fusion(f32[1024,1792]{1,0:T(8,128)} %get-tuple-element.173, bf16[4096,1792]{1,0:T(8,128)(2,1)} %get-tuple-element.185, s32[]{:T(128)S(6)} %select_n.26, pred[3072]{0:T(1024)(128)(4,1)S(1)} %dynamic-slice_compare_fusion.2, bf16[4096,1024]{1,0:T(8,128)(2,1)} %get-tuple-element.184, pred[]{:T(512)S(6)} %compare.3), kind=kOutput, calls=%fused_computation.4.clone.1 | convolution fusion | flops 11285299200 | bytes 31986176 | tf_op jit(solution)/shard_map/while/body/eval_jaxpr/dot_general | solution.py:35
  523.1 0.7 convert_reduce_fusion.2
  524.4 0.1 dynamic-slice_compare_fusion.2
  524.5 21.1 %select_add_fusion.2 = f32[1024,1792]{1,0:T(8,128)} fusion(f32[1024,1792]{1,0:T(8,128)} %get-tuple-element.173, bf16[4096,1792]{1,0:T(8,128)(2,1)} %get-tuple-element.185, s32[]{:T(128)S(6)} %select_n.26, pred[3072]{0:T(1024)(128)(4,1)S(1)} %dynamic-slice_compare_fusion.2, bf16[4096,1024]{1,0:T(8,128)(2,1)} %get-tuple-element.184, pred[]{:T(512)S(6)} %compare.3), kind=kOutput, calls=%fused_computation.4.clone.1 | convolution fusion | flops 11285299200 | bytes 31986176 | tf_op jit(solution)/shard_map/while/body/eval_jaxpr/dot_general | solution.py:35
  545.6 10.6 %multiply_add_fusion = (f32[1024,1792]{1,0:T(8,128)}, f32[1024,1792]{1,0:T(8,128)}) fusion(f32[1024,1792]{1,0:T(8,128)} %get-tuple-element.99, bf16[1,1024,1792]{2,1,0:T(8,128)(2,1)} %param.9), kind=kLoop, calls=%fused_computation.13 | loop fusion | flops 7340032 | bytes 25690112 | tf_op jit(solution)/shard_map/add | solution.py:41
  556.2 0.0 all-reduce.3.cloned.1.call-update
  556.2 281.0 %all-reduce.3.cloned.1.call-done = (f32[1024,1792]{1,0:T(8,128)}, f32[1024,1792]{1,0:T(8,128)}) async-done(((f32[1024,1792]{1,0:T(8,128)}, f32[1024,1792]{1,0:T(8,128)}), (f32[1024,1792]{1,0:T(8,128)}, f32[1024,1792]{1,0:T(8,128)})) %all-reduce.3.cloned.1.call-update) | async-done | bytes 14680080 | tf_op jit(solution)/shard_map/psum | solution.py:43
  837.2 8.0 divide_convert_fusion
  (1 shorter events, 0.0 us)
Async XLA Ops:
  15.0 164.8 %all-to-all-start = ((bf16[32,128,1024]{2,1,0:T(8,128)(2,1)}), bf16[32,128,1024]{2,1,0:T(8,128)(2,1)}, u32[]{:S(2)}, u32[]{:S(2)}) async-start(bf16[32,128,1024]{2,1,0:T(8,128)(2,1)} %bitcast.15), calls=%async_computation | async-start | bytes 16777216 | tf_op jit(solution)/shard_map/all_to_all | solution.py:22
  186.3 13.5 %copy-start = (s32[1,128]{1,0:T(1,128)S(1)}, s32[1,128]{1,0:T(1,128)}, u32[]{:S(2)}) copy-start(s32[1,128]{1,0:T(1,128)} %param.8) | copy-start | bytes 1540
  186.3 315.3 %all-to-all-start.1 = ((bf16[32,128,1792]{2,1,0:T(8,128)(2,1)}), bf16[32,128,1792]{2,1,0:T(8,128)(2,1)}, u32[]{:S(2)}, u32[]{:S(2)}) async-start(bf16[32,128,1792]{2,1,0:T(8,128)(2,1)} %bitcast.14), calls=%async_computation.1 | async-start | bytes 29360128 | tf_op jit(solution)/shard_map/all_to_all | solution.py:23
  199.7 637.5 %all-reduce.3.cloned.1.call-start = ((), (), s32[]{:S(2)}) async-start(), calls=%async_computation.2 | async-start | bytes 29360128 | tf_op jit(solution)/shard_map/psum | solution.py:43
Sparse Core Ops, SparseCore 0:
  556.3 280.8 all-reduce.2
where the time goes:
time: 852 us
  waiting for transfers between devices  429 us (50%)
  blocking collectives  302 us (35%)
  matrix products  41.2 us (5%)
  starting transfers between devices  24.8 us (3%)
  other arithmetic  20.2 us (2%)
  local copies, waits for them, and re-layouts  20 us (2%)
  between operations  13.4 us (2%)
    all_gather x1, blocking collectives, per_device(): owners = lax.all_gather(seq_ids[0], 'fsdp', axis=0, tiled=True)  302 us
    psum x1, waiting for transfers between devices, per_device(): numer_sum, denom_sum = lax.psum((numer, prior), 'mp')  281 us
    all_to_all x1, waiting for transfers between devices, per_device(): lax.all_to_all(act_send, 'fsdp', split_axis=0, concat_axis=1, tiled=True)[0]  148 us
    dot_general x2, matrix products, per_sequence(): lax.dot_general(act_window, masked, (((0,), (0,)), ((), ())), preferred_e...  41.2 us
  transfers between devices with their start and end apart: 3, of which 2 were waited for; matrix products, arithmetic and copies ran while one was open for 1% of the time, Pallas kernels for 0%

commit v1 on v0

--- a/solution.py
+++ b/solution.py
@@ -21,7 +21,9 @@
     grad_send = jnp.repeat(grad_blocks, row_blocks, axis=0)
     act_all = lax.all_to_all(act_send, "fsdp", split_axis=0, concat_axis=1, tiled=True)[0]
     grad_all = lax.all_to_all(grad_send, "fsdp", split_axis=0, concat_axis=1, tiled=True)[0]
-    owners = lax.all_gather(seq_ids[0], "fsdp", axis=0, tiled=True)
+    owners = jnp.concatenate(
+        lax.all_to_all(jnp.stack([seq_ids[0]] * lax.axis_size("fsdp")), "fsdp", 0, 0), axis=0
+    )
     total = owners.shape[0]
     longest = total // SEQS * 3 // 2
 

time: 852 us -> 814 us (0.955)
  blocking collectives: 302 us -> 0 us
  waiting for transfers between devices: 429 us -> 678 us
  starting transfers between devices: 24.8 us -> 38.8 us
    all_gather x1 -> x0, blocking collectives: 302 us -> none  [per_device(): owners = lax.all_gather(seq_ids[0], 'fsdp', axis=0, tiled=True)]
    all_to_all x1, waiting for transfers between devices: 0.01 us -> 270 us  [per_device(): lax.all_to_all(grad_send, 'fsdp', split_axis=0, concat_axis=1, tiled=True)]
    all_to_all x1, waiting for transfers between devices: 148 us -> 125 us  [per_device(): lax.all_to_all(act_send, 'fsdp', split_axis=0, concat_axis=1, tiled=True)[0]]
    all_to_all x0 -> x1, starting transfers between devices: none -> 11.2 us  [per_device(): lax.all_to_all(jnp.stack([seq_ids[0]] * lax.axis_size('fsdp')), 'fsdp', 0...]
    all_to_all x1, starting transfers between devices: 13.4 us -> 22.4 us  [per_device(): lax.all_to_all(grad_send, 'fsdp', split_axis=0, concat_axis=1, tiled=True)]
  transfers between devices with their start and end apart: 3 -> 4, of which waited for: 2 -> 4; matrix products, arithmetic and copies ran while one was open for 1% -> 1% of each run, Pallas kernels for 0% -> 0%
where the time goes in v1:
time: 814 us
  waiting for transfers between devices  678 us (83%)
  matrix products  41.2 us (5%)
  starting transfers between devices  38.8 us (5%)
  local copies, waits for them, and re-layouts  21.2 us (3%)
  other arithmetic  20.1 us (2%)
  between operations  13.4 us (2%)
    psum x1, waiting for transfers between devices, per_device(): numer_sum, denom_sum = lax.psum((numer, prior), 'mp')  278 us
    all_to_all x1, waiting for transfers between devices, per_device(): lax.all_to_all(grad_send, 'fsdp', split_axis=0, concat_axis=1, tiled=True)  270 us
    all_to_all x1, waiting for transfers between devices, per_device(): lax.all_to_all(act_send, 'fsdp', split_axis=0, concat_axis=1, tiled=True)[0]  125 us
    dot_general x2, matrix products, per_sequence(): lax.dot_general(act_window, masked, (((0,), (0,)), ((), ())), preferred_e...  41.2 us
    all_to_all x1, starting transfers between devices, per_device(): lax.all_to_all(grad_send, 'fsdp', split_axis=0, concat_axis=1, tiled=True)  22.4 us
  transfers between devices with their start and end apart: 4, of which 4 were waited for; matrix products, arithmetic and copies ran while one was open for 1% of the time, Pallas kernels for 0%

profile of v1, /device:TPU:1, one launch (start us, length us, event | category | flops | bytes accessed | tf_op | source)
XLA Modules:
  0.0 813.5 jit_solution(11673599420430862962)
XLA Ops:
  6.5 1.3 stack.3
  7.8 11.2 %all-to-all-start = ((s32[32,1,128]{2,1,0:T(1,128)}), s32[32,1,128]{2,1,0:T(1,128)S(1)}, u32[]{:S(2)}, u32[]{:S(2)}) async-start(s32[32,1,128]{2,1,0:T(1,128)} %stack.3), calls=%async_computation | async-start | bytes 32768 | tf_op jit(solution)/shard_map/all_to_all | solution.py:25
  19.0 3.0 copy.7
  22.0 1.2 copy.5
  23.2 4.4 all-to-all-done
  27.6 4.4 tile.4
  31.9 5.0 all-to-all-start.1
  36.9 3.6 reshape_squeeze.7
  40.5 1.4 copy.6
  41.9 124.7 %all-to-all-done.1 = bf16[32,128,1024]{2,1,0:T(8,128)(2,1)} async-done(((bf16[32,128,1024]{2,1,0:T(8,128)(2,1)}), bf16[32,128,1024]{2,1,0:T(8,128)(2,1)}, u32[]{:S(2)}, u32[]{:S(2)}) %all-to-all-start.1) | async-done | bytes 8388640 | tf_op jit(solution)/shard_map/all_to_all | solution.py:22
  166.7 6.4 broadcast_in_dim.26
  173.1 22.4 %all-to-all-start.2 = ((bf16[32,128,1792]{2,1,0:T(8,128)(2,1)}), bf16[32,128,1792]{2,1,0:T(8,128)(2,1)}, u32[]{:S(2)}, u32[]{:S(2)}) async-start(bf16[32,128,1792]{2,1,0:T(8,128)(2,1)} %bitcast.15), calls=%async_computation.2 | async-start | bytes 29360128 | tf_op jit(solution)/shard_map/all_to_all | solution.py:23
  195.5 0.2 all-reduce.3.cloned.1.call-start
  195.7 270.4 %all-to-all-done.2 = bf16[32,128,1792]{2,1,0:T(8,128)(2,1)} async-done(((bf16[32,128,1792]{2,1,0:T(8,128)(2,1)}), bf16[32,128,1792]{2,1,0:T(8,128)(2,1)}, u32[]{:S(2)}, u32[]{:S(2)}) %all-to-all-start.2) | async-done | bytes 14680096 | tf_op jit(solution)/shard_map/all_to_all | solution.py:23
  466.2 43.9 %while.14 = (s32[]{:T(128)}, f32[1024,1792]{1,0:T(8,128)}, s32[4096]{0:T(1024)S(1)}, bf16[4096,1024]{1,0:T(8,128)(2,1)}, bf16[4096,1792]{1,0:T(8,128)(2,1)}, /*index=5*/s32[]{:T(128)}, s32[]{:T(128)}, s32[]{:T(128)}, s32[]{:T(128)}) while((s32[]{:T(128)}, f32[1024,1792]{1,0:T(8,128)}, s32[4096]{0:T(1024)S(1)}, ...), condition=%wide.region_2.3_spmd.clone, body=%wide.region_0.2_spmd.clone.sunk | while | flops 11285314560 | bytes 32018084 | solution.py:42
  466.2 0.7 convert_reduce_fusion.2
  467.5 0.1 dynamic-slice_compare_fusion.2
  467.5 20.1 %select_add_fusion.2 = f32[1024,1792]{1,0:T(8,128)} fusion(f32[1024,1792]{1,0:T(8,128)} %get-tuple-element.173, bf16[4096,1792]{1,0:T(8,128)(2,1)} %get-tuple-element.185, s32[]{:T(128)S(6)} %select_n.26, pred[3072]{0:T(1024)(128)(4,1)S(1)} %dynamic-slice_compare_fusion.2, bf16[4096,1024]{1,0:T(8,128)(2,1)} %get-tuple-element.184, pred[]{:T(512)S(6)} %compare.3), kind=kOutput, calls=%fused_computation.4.clone.1 | convolution fusion | flops 11285299200 | bytes 31986176 | tf_op jit(solution)/shard_map/while/body/eval_jaxpr/dot_general | solution.py:37
  487.6 0.7 convert_reduce_fusion.2
  488.9 0.1 dynamic-slice_compare_fusion.2
  489.0 21.1 %select_add_fusion.2 = f32[1024,1792]{1,0:T(8,128)} fusion(f32[1024,1792]{1,0:T(8,128)} %get-tuple-element.173, bf16[4096,1792]{1,0:T(8,128)(2,1)} %get-tuple-element.185, s32[]{:T(128)S(6)} %select_n.26, pred[3072]{0:T(1024)(128)(4,1)S(1)} %dynamic-slice_compare_fusion.2, bf16[4096,1024]{1,0:T(8,128)(2,1)} %get-tuple-element.184, pred[]{:T(512)S(6)} %compare.3), kind=kOutput, calls=%fused_computation.4.clone.1 | convolution fusion | flops 11285299200 | bytes 31986176 | tf_op jit(solution)/shard_map/while/body/eval_jaxpr/dot_general | solution.py:37
  510.1 10.6 %multiply_add_fusion = (f32[1024,1792]{1,0:T(8,128)}, f32[1024,1792]{1,0:T(8,128)}) fusion(f32[1024,1792]{1,0:T(8,128)} %get-tuple-element.99, bf16[1,1024,1792]{2,1,0:T(8,128)(2,1)} %param.9), kind=kLoop, calls=%fused_computation.13 | loop fusion | flops 7340032 | bytes 25690112 | tf_op jit(solution)/shard_map/add | solution.py:43
  520.7 0.0 all-reduce.3.cloned.1.call-update
  520.7 278.0 %all-reduce.3.cloned.1.call-done = (f32[1024,1792]{1,0:T(8,128)}, f32[1024,1792]{1,0:T(8,128)}) async-done(((f32[1024,1792]{1,0:T(8,128)}, f32[1024,1792]{1,0:T(8,128)}), (f32[1024,1792]{1,0:T(8,128)}, f32[1024,1792]{1,0:T(8,128)})) %all-reduce.3.cloned.1.call-update) | async-done | bytes 14680080 | tf_op jit(solution)/shard_map/psum | solution.py:45
  798.7 8.0 divide_convert_fusion
  (1 shorter events, 0.0 us)
Async XLA Ops:
  7.8 19.8 %all-to-all-start = ((s32[32,1,128]{2,1,0:T(1,128)}), s32[32,1,128]{2,1,0:T(1,128)S(1)}, u32[]{:S(2)}, u32[]{:S(2)}) async-start(s32[32,1,128]{2,1,0:T(1,128)} %stack.3), calls=%async_computation | async-start | bytes 32768 | tf_op jit(solution)/shard_map/all_to_all | solution.py:25
  31.9 134.8 %all-to-all-start.1 = ((bf16[32,128,1024]{2,1,0:T(8,128)(2,1)}), bf16[32,128,1024]{2,1,0:T(8,128)(2,1)}, u32[]{:S(2)}, u32[]{:S(2)}) async-start(bf16[32,128,1024]{2,1,0:T(8,128)(2,1)} %bitcast.16), calls=%async_computation.1 | async-start | bytes 16777216 | tf_op jit(solution)/shard_map/all_to_all | solution.py:22
  173.1 293.1 %all-to-all-start.2 = ((bf16[32,128,1792]{2,1,0:T(8,128)(2,1)}), bf16[32,128,1792]{2,1,0:T(8,128)(2,1)}, u32[]{:S(2)}, u32[]{:S(2)}) async-start(bf16[32,128,1792]{2,1,0:T(8,128)(2,1)} %bitcast.15), calls=%async_computation.2 | async-start | bytes 29360128 | tf_op jit(solution)/shard_map/all_to_all | solution.py:23
  195.5 603.2 %all-reduce.3.cloned.1.call-start = ((), (), s32[]{:S(2)}) async-start(), calls=%async_computation.3 | async-start | bytes 29360128 | tf_op jit(solution)/shard_map/psum | solution.py:45
Sparse Core Ops, SparseCore 0:
  520.8 277.7 all-reduce.2
